TPU v7x, 32 devices: a whole 2x2x4 slice. The times are simulated.
32 devices in a mesh: rows: 8 (over z, x), strips: 4 (over y, core).
Axes of the slice: x: 2, y: 2, z: 4, core: 2. Of those that a mesh axis runs over, the one named last changes fastest.
Arguments:
- tokens: bfloat16 [8, 24, 64, 1280], P('rows', None, 'strips'), may hold values from -8 to 8
- stale_kv: bfloat16 [8, 2, 1536, 1280], P('rows', None, 'strips'), may hold values from -180 to 180
- stale_moments: float32 [8, 4, 2, 32], P('rows', 'strips'), as said below
- norm_gain: float32 [1280], replicated, may hold values from 0.1 to 1.9
- norm_bias: float32 [1280], replicated, may hold values from -3 to 3
- w_query: bfloat16 [1280, 1280], P('rows'), may hold values from -0.33398438 to 0.33398438
- w_key: bfloat16 [1280, 1280], P('rows'), may hold values from -0.1953125 to 0.1953125
- w_value: bfloat16 [1280, 1280], P('rows'), may hold values from -0.15625 to 0.15625
- w_out: bfloat16 [1280, 1280], P('rows'), may hold values from -0.33398438 to 0.33398438
Outputs:
- attended: bfloat16 [8, 24, 64, 1280], P('rows', None, 'strips')
- fresh_kv: bfloat16 [8, 2, 1536, 1280], P('rows', None, 'strips')
- fresh_sums: float32 [8, 4, 32], P('rows', 'strips')
- fresh_squares: float32 [8, 4, 32], P('rows', 'strips')
Inputs may be any that keep to these rules, and one draw needn't show every extreme that they name: `stale_moments`: each strip's entries are a sum of 15360 values and the sum of their squares.
All inputs are finite; a program needn't handle non-finite values.
Results may differ from a plain program's by a relative error of at most 0.0075.
The roundings to bfloat16 on the way count: a program that leaves them out, or rounds other values in their place, can miss the bound.
Values may be sent and summed in bfloat16 or wider, within the bound.
No kernel may reach another device: no remote copies, remote signals or barrier semaphores. Data moves between devices by JAX's collectives and lax.ppermute only.
A program may use at most 128 MiB of HBM per device.

v0:
```python
import jax
import jax.numpy as jnp
from jax import lax
from jax.sharding import PartitionSpec as P

HEADS = 20
HEAD = 64


def fold_keys(carry, piece, query_heads, own_start, own_count):
    top_score, total, weighted = carry
    count = piece.shape[1]
    heads = query_heads.shape[0]
    size = query_heads.shape[2]
    keys_part = piece[0].reshape(count, heads, size).transpose(1, 0, 2)
    vals_part = piece[1].reshape(count, heads, size).transpose(1, 0, 2)
    places = jnp.arange(count, dtype=jnp.int32)
    inside = (places >= own_start) & (places < own_start + own_count)

    def per_head(items):
        head_top, head_total, head_sum, head_query, head_keys, head_vals = items
        scores = jnp.dot(head_query, head_keys.T, preferred_element_type=jnp.float32)
        scores = jnp.where(inside[None, :], jnp.float32(-1e30), scores)
        new_top = jnp.maximum(head_top, scores.max(axis=-1))
        factor = jnp.exp(head_top - new_top)
        weights = jnp.exp(scores - new_top[:, None])
        upper = weights.astype(jnp.bfloat16)
        lower = (weights - upper.astype(jnp.float32)).astype(jnp.bfloat16)
        head_total = head_total * factor + weights.sum(axis=-1)
        product = jnp.dot(upper, head_vals, preferred_element_type=jnp.float32) + jnp.dot(
            lower, head_vals, preferred_element_type=jnp.float32
        )
        head_sum = head_sum * factor[:, None] + product
        return (new_top, head_total, head_sum)

    return lax.map(per_head, (top_score, total, weighted, query_heads, keys_part, vals_part))


def shards(tokens, stale_kv, stale_moments, norm_gain, norm_bias, w_query, w_key, w_value, w_out):
    band, width, chans = (tokens.shape[1], tokens.shape[2], tokens.shape[3])
    tok_count = band * width
    groups = stale_moments.shape[3]
    per_group = chans // groups
    strips = lax.axis_size("strips")
    flat = tokens.reshape(tok_count, chans).astype(jnp.float32)
    grouped = flat.reshape(tok_count, groups, per_group)
    fresh = jnp.stack([grouped.sum(axis=(0, 2)), (grouped * grouped).sum(axis=(0, 2))])
    own_moments = stale_moments[0]
    own_kv = stale_kv[0]
    totals = lax.psum(own_moments[0], "strips")
    mixed = totals - own_moments[0] + fresh
    count = float(tok_count * strips * per_group)
    mean = mixed[0] / count
    var = mixed[1] / count - mean * mean
    rstd = lax.rsqrt(var + 1e-05)
    normed = ((grouped - mean[None, :, None]) * rstd[None, :, None]).reshape(tok_count, chans)
    normed = (normed * norm_gain + norm_bias).astype(jnp.bfloat16)
    strip_index = lax.axis_index("strips")
    pieces = (
        lax.all_gather(w_query, "rows", axis=0, tiled=True),
        lax.all_gather(w_key, "rows", axis=0, tiled=True),
        lax.all_gather(w_value, "rows", axis=0, tiled=True),
    )
    columns = normed
    query_sum, key_sum, value_sum = tuple(
        (jnp.dot(columns, piece, preferred_element_type=jnp.float32) for piece in pieces)
    )
    query = (query_sum * (1.0 / HEAD**0.5)).astype(jnp.bfloat16)
    key = key_sum.astype(jnp.bfloat16)
    value = value_sum.astype(jnp.bfloat16)
    fresh_kv = jnp.stack([key, value])
    query_heads = query.reshape(tok_count, HEADS, HEAD).transpose(1, 0, 2)
    start_carry = (
        jnp.full((HEADS, tok_count), -1e30, jnp.float32),
        jnp.zeros((HEADS, tok_count), jnp.float32),
        jnp.zeros((HEADS, tok_count, HEAD), jnp.float32),
    )
    carry = fold_keys(start_carry, fresh_kv, query_heads, 0, 0)
    own_start = strip_index * tok_count
    top_score, total, weighted = fold_keys(
        carry,
        lax.all_gather(own_kv, "strips", axis=1, tiled=True),
        query_heads,
        own_start,
        tok_count,
    )
    heads_out = (
        (weighted / total[..., None])
        .transpose(1, 0, 2)
        .reshape(tok_count, HEADS * HEAD)
        .astype(jnp.bfloat16)
    )
    columns = heads_out
    attended = jnp.dot(
        columns,
        lax.all_gather(w_out, "rows", axis=0, tiled=True),
        preferred_element_type=jnp.float32,
    )
    attended = attended.astype(jnp.bfloat16)
    return (
        attended.reshape(1, band, width, chans),
        fresh_kv[None],
        fresh[0][None, None],
        fresh[1][None, None],
    )


def solution(mesh):
    in_specs = (
        P("rows", None, "strips", None),
        P("rows", None, "strips", None),
        P("rows", "strips", None, None),
        P(),
        P(),
        P("rows", None),
        P("rows", None),
        P("rows", None),
        P("rows", None),
    )
    out_specs = (
        P("rows", None, "strips", None),
        P("rows", None, "strips", None),
        P("rows", "strips", None),
        P("rows", "strips", None),
    )
    return jax.shard_map(shards, mesh=mesh, in_specs=in_specs, out_specs=out_specs, check_vma=False)
```

profile of v0, /device:TPU:0, one launch (start us, length us, event | category | flops | bytes accessed | tf_op | source)
XLA Modules:
  0.0 416.8 jit_solution(2687440719954865516)
XLA Ops:
  9.4 4.0 copy.32
  15.1 8.4 %psum.7 = f32[2,32]{1,0:T(2,128)S(1)} all-reduce(f32[2,32]{1,0:T(2,128)S(1)} %bitcast.135), channel_id=1, replica_groups=mesh['rows'=8,'strips'=4] {'strips'}, use_global_device_ids=true, to_apply=%region_0.0 | all-reduce | flops 64 | bytes 512 | tf_op jit(solution)/shard_map/psum | solution.py:50
  24.5 49.8 %all-gather.7.cloned.1.call-done = bf16[1280,1280]{1,0:T(8,128)(2,1)} async-done(((bf16[160,1280]{1,0:T(8,128)(2,1)}), bf16[1280,1280]{1,0:T(8,128)(2,1)}) %all-gather.7.cloned.1.call-update) | async-done | bytes 3276816 | tf_op jit(solution)/shard_map/all_gather | solution.py:60
  74.4 3.4 fusion.49
  79.5 57.2 %all-gather.9.cloned.1.call-done = bf16[1280,1280]{1,0:T(8,128)(2,1)} async-done(((bf16[160,1280]{1,0:T(8,128)(2,1)}), bf16[1280,1280]{1,0:T(8,128)(2,1)}) %all-gather.9.cloned.1.call-update) | async-done | bytes 3276816 | tf_op jit(solution)/shard_map/all_gather | solution.py:61
  136.7 3.7 convolution_convert_fusion.2
  141.7 57.4 %all-gather.11.cloned.1.call-done = bf16[1280,1280]{1,0:T(8,128)(2,1)} async-done(((bf16[160,1280]{1,0:T(8,128)(2,1)}), bf16[1280,1280]{1,0:T(8,128)(2,1)}) %all-gather.11.cloned.1.call-update) | async-done | bytes 3276816 | tf_op jit(solution)/shard_map/all_gather | solution.py:62
  199.1 4.7 %convolution_convert_fusion.1 = bf16[384,1280]{1,0:T(8,128)(2,1)} fusion(bf16[384,1280]{1,0:T(8,128)(2,1)} %copy-done.2, bf16[1280,1280]{1,0:T(8,128)(2,1)} %all-gather.11.cloned.1.call-done), kind=kOutput, calls=%fused_computation.65 | convolution fusion | flops 1258782720 | bytes 5242880 | tf_op jit(solution)/shard_map/dot_general | solution.py:66
  203.7 2.2 copy.28
  206.0 1.5 broadcast.114.clone
  207.5 82.3 %while.28 = (s32[]{:T(128)}, f32[20,384]{1,0:T(8,128)S(1)}, f32[20,384]{1,0:T(8,128)S(1)}, f32[20,384,64]{1,2,0:T(8,128)}, bf16[20,384,64]{2,1,0:T(8,128)(2,1)S(...) while((s32[]{:T(128)}, f32[20,384]{1,0:T(8,128)S(1)}, ...), condition=%wide.region_8.9_spmd, body=%wide.region_5.8_spmd.sunk | while | flops 58148352 | bytes 2930277 | solution.py:36
  209.7 1.7 fusion.90
  213.8 1.7 fusion.90
  217.9 1.7 fusion.90
  222.0 1.7 fusion.90
  226.1 1.7 fusion.90
  230.2 1.7 fusion.90
  234.4 1.7 fusion.90
  238.5 1.7 fusion.90
  242.6 1.7 fusion.90
  246.7 1.7 fusion.90
  250.8 1.7 fusion.90
  254.9 1.7 fusion.90
  259.0 1.7 fusion.90
  263.2 1.7 fusion.90
  267.3 1.7 fusion.90
  271.4 1.7 fusion.90
  275.5 1.7 fusion.90
  279.6 1.7 fusion.90
  283.8 1.7 fusion.90
  287.9 1.7 fusion.90
  289.9 3.4 maximum_bitcast_fusion
  293.2 5.6 %fusion.58 = (bf16[1,1,1536,1280]{2,3,1,0:T(8,128)(2,1)}, bf16[1,1,1536,1280]{2,3,1,0:T(8,128)(2,1)}) fusion(bf16[1,2,1536,1280]{2,3,1,0:T(8,128)(2,1)} %all-gather.15.cloned.1.call-done), kind=kLoop, calls=%fused_computation.83 | loop fusion | bytes 15728640 | tf_op jit(solution)/shard_map/slice | solution.py:16
  299.0 106.6 %while.29 = (s32[]{:T(128)}, f32[20,384]{1,0:T(8,128)S(1)}, f32[20,384,64]{1,2,0:T(8,128)S(1)}, f32[20,384]{1,0:T(8,128)S(1)}, f32[20,384]{1,0:T(8,128)S(1)}, /*...) while((s32[]{:T(128)}, f32[20,384]{1,0:T(8,128)S(1)}, ...), condition=%wide.region_12.13_spmd.clone, body=%wide.region_9.12_spmd.clone.sunk | while | flops 233060352 | bytes 10554513 | solution.py:36
  300.6 1.5 fusion.99
  302.2 1.6 fusion.100
  307.5 1.6 fusion.100
  311.3 1.5 fusion.99
  312.8 1.6 fusion.100
  318.2 1.6 fusion.100
  323.5 1.6 fusion.100
  327.3 1.5 fusion.99
  328.8 1.6 fusion.100
  332.6 1.5 fusion.99
  334.2 1.6 fusion.100
  337.9 1.5 fusion.99
  339.5 1.6 fusion.100
  343.3 1.5 fusion.99
  344.8 1.6 fusion.100
  348.6 1.5 fusion.99
  350.2 1.6 fusion.100
  353.9 1.5 fusion.99
  355.5 1.6 fusion.100
  359.3 1.5 fusion.99
  360.8 1.6 fusion.100
  366.1 1.6 fusion.100
  371.5 1.6 fusion.100
  376.8 1.6 fusion.100
  382.1 1.6 fusion.100
  387.5 1.6 fusion.100
  392.8 1.6 fusion.100
  398.1 1.6 fusion.100
  403.5 1.6 fusion.100
  405.9 4.4 %convolution_convert_fusion = bf16[384,1280]{1,0:T(8,128)(2,1)} fusion(bf16[384,1280]{0,1:T(8,128)(2,1)S(1)} %bitcast.134, bf16[1280,1280]{1,0:T(8,128)(2,1)} %all-gather.13.cloned.1.call-done), kind=kOutput, calls=%fused_computation.64 | convolution fusion | flops 1258782720 | bytes 5242880 | tf_op jit(solution)/shard_map/dot_general | solution.py:94
  (360 shorter events, 114.8 us)
Async XLA Ops:
  7.2 67.2 %all-gather.7.cloned.1.call-start = ((), (), s32[]{:S(2)}) async-start(), calls=%async_computation | async-start | bytes 3686400 | tf_op jit(solution)/shard_map/all_gather | solution.py:60
  7.9 128.8 %all-gather.9.cloned.1.call-start = ((), (), s32[]{:S(2)}) async-start(), calls=%async_computation.1 | async-start | bytes 3686400 | tf_op jit(solution)/shard_map/all_gather | solution.py:61
  8.6 190.4 %all-gather.11.cloned.1.call-start = ((), (), s32[]{:S(2)}) async-start(), calls=%async_computation.2 | async-start | bytes 3686400 | tf_op jit(solution)/shard_map/all_gather | solution.py:62
  9.4 283.9 %all-gather.15.cloned.1.call-start = ((), (), s32[]{:S(2)}) async-start(), calls=%async_computation.4 | async-start | bytes 9830400 | tf_op jit(solution)/shard_map/all_gather | solution.py:82
  13.4 1.2 copy-start.1
  13.4 1.7 copy-start.5
  13.4 10.7 %copy-start.3 = (f32[1280]{0:T(1024)S(1)}, f32[1280]{0:T(1024)}, u32[]{:S(2)}) copy-start(f32[1280]{0:T(1024)} %param.17) | copy-start | bytes 15364
  13.4 10.7 %copy-start.4 = (f32[1280]{0:T(1024)S(1)}, f32[1280]{0:T(1024)}, u32[]{:S(2)}) copy-start(f32[1280]{0:T(1024)} %param.16) | copy-start | bytes 15364
  13.5 392.4 %all-gather.13.cloned.1.call-start = ((), (), s32[]{:S(2)}) async-start(), calls=%async_computation.3 | async-start | bytes 3686400 | tf_op jit(solution)/shard_map/all_gather | solution.py:96
  23.6 54.1 %copy-start.6 = (f32[32]{0:T(128)}, f32[32]{0:T(128)S(1)}, u32[]{:S(2)}) copy-start(f32[32]{0:T(128)S(1)} %reduce_sum.58) | copy-start | bytes 388
  23.7 54.0 %copy-start.7 = (f32[32]{0:T(128)}, f32[32]{0:T(128)S(1)}, u32[]{:S(2)}) copy-start(f32[32]{0:T(128)S(1)} %reduce_sum.61) | copy-start | bytes 388
  24.5 53.2 %copy-start.2 = (bf16[384,1280]{1,0:T(8,128)(2,1)}, bf16[384,1280]{1,0:T(8,128)(2,1)S(1)}, u32[]{:S(2)}) copy-start(bf16[384,1280]{1,0:T(8,128)(2,1)S(1)} %fusion.53) | copy-start | bytes 2949124
  289.9 3.4 copy-start
Sparse Core Ops, SparseCore 0:
  10.2 64.1 all-gather.6
  76.5 60.1 all-gather.8
  138.9 60.1 all-gather.10
  200.5 53.8 all-gather.14
  256.4 61.4 all-gather.12
where the time goes:
time: 422 us; the launch traced here: 417 us
  matrix products  186 us (44%)
  waiting for transfers between devices  167 us (40%)
  local copies, waits for them, and re-layouts  21.4 us (5%)
  other arithmetic  17.5 us (4%)
  between operations  14 us (3%)
  blocking collectives  8.4 us (2%)
    dot_general x40, matrix products, per_head(): jnp.dot(lower, head_vals, preferred_element_type=jnp.float32)  66.4 us
    all_gather x1, waiting for transfers between devices, shards(): lax.all_gather(w_value, 'rows', axis=0, tiled=True)  57.4 us
    all_gather x1, waiting for transfers between devices, shards(): lax.all_gather(w_key, 'rows', axis=0, tiled=True)  57.2 us
    dot_general x40, matrix products, per_head(): jnp.dot(head_query, head_keys.T, preferred_element_type=jnp.float32)  52.4 us
    dot_general x40, matrix products, per_head(): jnp.dot(upper, head_vals, preferred_element_type=jnp.float32)  51.4 us
    all_gather x1, waiting for transfers between devices, shards(): lax.all_gather(w_query, 'rows', axis=0, tiled=True)  49.8 us
    reduce_sum x40, other arithmetic, per_head(): head_total = head_total * factor + weights.sum(axis=-1)  11.8 us
    dot_general x3, matrix products, shards(): jnp.dot(columns, piece, preferred_element_type=jnp.float32)  11.7 us
  transfers between devices with their start and end apart: 5, of which 3 were waited for; matrix products, arithmetic and copies ran while one was open for 53% of the time, Pallas kernels for 0%

commit v1 on v0

v1 whole, which is shorter than its diff:
```python
import functools

import jax
import jax.numpy as jnp
from jax import lax
from jax.experimental import pallas as pl
from jax.experimental.pallas import tpu as pltpu
from jax.sharding import PartitionSpec as P


HEAD = 64
PAIR = 2 * HEAD
EPS = 1e-05


def group_matrix(chans, groups):
    per = chans // groups
    first = lax.broadcasted_iota(jnp.int32, (chans, groups), 1) * per
    place = lax.broadcasted_iota(jnp.int32, (chans, groups), 0)
    return jnp.where((place >= first) & (place < first + per), 1.0, 0.0).astype(jnp.bfloat16)


def exact_dot(rows, member, dims):
    high = rows.astype(jnp.bfloat16)
    rest = rows - high.astype(jnp.float32)
    middle = rest.astype(jnp.bfloat16)
    low = (rest - middle.astype(jnp.float32)).astype(jnp.bfloat16)
    parts = [
        lax.dot_general(p, member, (dims, ((), ())), preferred_element_type=jnp.float32)
        for p in (high, middle, low)
    ]
    return (parts[2] + parts[1]) + parts[0]


def norm_kernel(count, tok_ref, other_ref, gain_ref, bias_ref, fresh_ref, out_ref):
    chans = tok_ref.shape[1]
    groups = fresh_ref.shape[1]
    values = tok_ref[...].astype(jnp.float32)
    sums = jnp.sum(values, axis=0, keepdims=True)
    squares = jnp.sum(values * values, axis=0, keepdims=True)
    row = lax.broadcasted_iota(jnp.int32, (8, chans), 0)
    both = jnp.where(row == 0, sums, jnp.where(row == 1, squares, 0.0))
    member = group_matrix(chans, groups)
    fresh = exact_dot(both, member, ((1,), (0,)))
    fresh_ref[...] = fresh[0:2]
    mixed = other_ref[...] + fresh[0:2]
    mean = mixed[0:1] / count
    var = mixed[1:2] / count - mean * mean
    rstd = lax.rsqrt(var + EPS)
    grow = lax.broadcasted_iota(jnp.int32, (8, groups), 0)
    stats = jnp.where(grow == 0, mean, jnp.where(grow == 1, rstd, 0.0))
    wide = exact_dot(stats, member, ((1,), (1,)))
    normed = (values - wide[0:1]) * wide[1:2]
    gain = gain_ref[...].reshape(1, chans)
    bias = bias_ref[...].reshape(1, chans)
    out_ref[...] = (normed * gain + bias).astype(out_ref.dtype)


def normalize(flat, others, gain, bias, count):
    tokens, chans = flat.shape
    groups = others.shape[1]
    return pl.pallas_call(
        functools.partial(norm_kernel, count),
        out_shape=(
            jax.ShapeDtypeStruct((2, groups), jnp.float32),
            jax.ShapeDtypeStruct((tokens, chans), jnp.bfloat16),
        ),
        cost_estimate=pl.CostEstimate(
            flops=8 * tokens * chans, bytes_accessed=4 * tokens * chans, transcendentals=0
        ),
        compiler_params=pltpu.CompilerParams(vmem_limit_bytes=12 << 20),
        name="normalize",
    )(flat, others, gain, bias)


def project_kernel(plan, scale, split, *refs):
    ids_ref, left_ref, right_ref = refs[:3]
    pieces = refs[3 : 3 + len(plan)]
    mine_ref, sent_ref, tokens_ref, held_ref, sem_ref = refs[3 + len(plan) :]
    shards, rows, cols = held_ref.shape
    copies = [
        pltpu.make_async_copy(left_ref, tokens_ref.at[0], sem_ref.at[0]),
        pltpu.make_async_copy(right_ref, tokens_ref.at[1], sem_ref.at[1]),
    ]
    at = 0
    for piece, offset in zip(pieces, plan):
        for k in range(piece.shape[0]):
            copies.append(
                pltpu.make_async_copy(
                    piece.at[k, offset], held_ref.at[ids_ref[at]], sem_ref.at[2 + at]
                )
            )
            at += 1

    @pl.when(pl.program_id(0) == 0)
    def _():
        for copy in copies:
            copy.start()
        for copy in copies:
            copy.wait()

    def compute(side, out_ref):
        if split:
            half = shards // 2
            core = ids_ref[at]
            depth = half * rows
            low = held_ref[pl.ds(core * half, half)].reshape(depth, cols)
            high = held_ref[pl.ds((1 - core) * half, half)].reshape(depth, cols)
            total = jnp.dot(tokens_ref[0, side], low, preferred_element_type=jnp.float32)
            total += jnp.dot(tokens_ref[1, 1 - side], high, preferred_element_type=jnp.float32)
        else:
            whole = held_ref[...].reshape(shards * rows, cols)
            total = jnp.dot(tokens_ref[side], whole, preferred_element_type=jnp.float32)
        out_ref[...] = (total * scale).astype(out_ref.dtype)

    @pl.when(pl.program_id(0) == 0)
    def _():
        compute(1, sent_ref)

    @pl.when(pl.program_id(0) == 1)
    def _():
        compute(0, mine_ref)


def project(left, right, pieces, ids, scale=1.0, split=False):
    tokens = left.shape[-2]
    _, _, rows, cols = pieces[0][0].shape
    shards = sum(piece.shape[0] for piece, _ in pieces)
    depth = shards * rows
    if rows % 16:
        order = jnp.argsort(ids[:shards])
        stacked = jnp.concatenate([p[:, o : o + 1] for p, o in pieces])
        merged = jnp.take(stacked, order, axis=0).reshape(2, 1, depth // 2, cols)
        ids = jnp.concatenate([jnp.arange(2, dtype=jnp.int32), ids[shards:]])
        pieces, shards, rows = [(merged, 0)], 2, depth // 2
    hbm = pl.BlockSpec(memory_space=pl.ANY)
    out = jax.ShapeDtypeStruct((tokens, cols), jnp.bfloat16)
    whole = pl.BlockSpec((tokens, cols), lambda i: (0, 0))
    return pl.pallas_call(
        functools.partial(project_kernel, tuple(o for _, o in pieces), scale, split),
        grid=(2,),
        out_shape=(out, out),
        in_specs=[pl.BlockSpec(memory_space=pltpu.SMEM)] + [hbm] * (2 + len(pieces)),
        out_specs=(whole, whole),
        scratch_shapes=[
            pltpu.VMEM((2, *left.shape), jnp.bfloat16),
            pltpu.VMEM((shards, rows, cols), jnp.bfloat16),
            pltpu.SemaphoreType.DMA((shards + 2,)),
        ],
        cost_estimate=pl.CostEstimate(
            flops=4 * tokens * depth * cols,
            bytes_accessed=2 * (depth * cols + 4 * tokens * cols),
            transcendentals=0,
        ),
        compiler_params=pltpu.CompilerParams(vmem_limit_bytes=12 << 20),
    )(ids, left, right, *[p for p, _ in pieces])


def both_heads(query, keys, vals):
    tokens = query.shape[0]
    low = lax.broadcasted_iota(jnp.int32, (tokens, PAIR), 1) < HEAD
    zero = jnp.zeros_like(query)
    stacked = jnp.concatenate([jnp.where(low, query, zero), jnp.where(low, zero, query)])
    scores = lax.dot_general(
        stacked, keys, (((1,), (1,)), ((), ())), preferred_element_type=jnp.float32
    )
    top = jnp.max(scores, axis=-1, keepdims=True)
    weights = jnp.exp(scores - top).astype(jnp.bfloat16)
    summed = jnp.dot(
        weights,
        jnp.concatenate([vals, jnp.ones_like(vals)], axis=1),
        preferred_element_type=jnp.float32,
    )
    return (
        jnp.where(low, top[:tokens], top[tokens:]),
        jnp.where(low, summed[:tokens, :PAIR], summed[tokens:, :PAIR]),
        jnp.where(low, summed[:tokens, PAIR:], summed[tokens:, PAIR:]),
    )


def stale_kernel(
    core_ref, q0_ref, q1_ref, near_ref, own_ref, far_ref, diag_ref, top_ref, sum_ref, total_ref
):
    for side, (q_ref, first) in enumerate(((q0_ref, near_ref), (q1_ref, own_ref))):
        keys = jnp.concatenate([first[0], far_ref[0], diag_ref[0]])
        vals = jnp.concatenate([first[1], far_ref[1], diag_ref[1]])
        top_ref[side], sum_ref[side], total_ref[side] = both_heads(q_ref[...], keys, vals)


def fresh_kernel(
    q0_ref, q1_ref, k0_ref, k1_ref, v0_ref, v1_ref, top_ref, sum_ref, total_ref, out_ref
):
    for side, (q_ref, k_ref, v_ref) in enumerate(
        ((q0_ref, k0_ref, v0_ref), (q1_ref, k1_ref, v1_ref))
    ):
        here, summed, total = both_heads(q_ref[...], k_ref[...], v_ref[...])
        before = top_ref[side]
        top = jnp.maximum(here, before)
        new, old = jnp.exp(here - top), jnp.exp(before - top)
        summed = summed * new + sum_ref[side] * old
        total = total * new + total_ref[side] * old
        out_ref[side] = (summed / total).astype(out_ref.dtype)


def attend_stale(core, queries, near, own, far, diag):
    tokens, cols = queries[0].shape
    pairs = cols // PAIR
    flat = pl.BlockSpec((tokens, PAIR), lambda p, c: (0, p))
    wide = pl.BlockSpec((2, tokens, PAIR), lambda p, c: (0, 0, p))
    mine = pl.BlockSpec((2, tokens, PAIR), lambda p, c: (0, 0, c[0] * pairs + p))
    return pl.pallas_call(
        stale_kernel,
        grid_spec=pltpu.PrefetchScalarGridSpec(
            num_scalar_prefetch=1,
            grid=(pairs,),
            in_specs=[flat, flat, wide, mine, wide, wide],
            out_specs=(wide,) * 3,
        ),
        out_shape=(jax.ShapeDtypeStruct((2, tokens, cols), jnp.float32),) * 3,
        cost_estimate=pl.CostEstimate(
            flops=6 * tokens * tokens * cols * 16,
            bytes_accessed=40 * tokens * cols,
            transcendentals=6 * tokens * tokens * cols // HEAD,
        ),
        compiler_params=pltpu.CompilerParams(vmem_limit_bytes=20 << 20),
        name="attend_stale",
    )(core, *queries, near, own, far, diag)


def attend_fresh(queries, keys, vals, carry):
    tokens, cols = queries[0].shape
    pairs = cols // PAIR
    flat = pl.BlockSpec((tokens, PAIR), lambda p: (0, p))
    wide = pl.BlockSpec((2, tokens, PAIR), lambda p: (0, 0, p))
    return pl.pallas_call(
        fresh_kernel,
        grid=(pairs,),
        in_specs=[flat] * 6 + [wide] * 3,
        out_specs=wide,
        out_shape=jax.ShapeDtypeStruct((2, tokens, cols), jnp.bfloat16),
        cost_estimate=pl.CostEstimate(
            flops=2 * tokens * tokens * cols * 16,
            bytes_accessed=40 * tokens * cols,
            transcendentals=2 * tokens * tokens * cols // HEAD,
        ),
        compiler_params=pltpu.CompilerParams(vmem_limit_bytes=12 << 20),
        name="attend_fresh",
    )(*queries, *keys, *vals, *carry)


def join_kernel(core_ref, mine_ref, other_ref, out_ref):
    own = pl.program_id(0) == core_ref[0]

    @pl.when(own)
    def _():
        out_ref[...] = mine_ref[...]

    @pl.when(jnp.logical_not(own))
    def _():
        out_ref[...] = other_ref[...]


def join(core, mine, other):
    tokens, cols = mine.shape
    whole = pl.BlockSpec((tokens, cols), lambda j, c: (0, 0))
    return pl.pallas_call(
        join_kernel,
        grid_spec=pltpu.PrefetchScalarGridSpec(
            num_scalar_prefetch=1,
            grid=(2,),
            in_specs=[whole, whole],
            out_specs=pl.BlockSpec((tokens, cols), lambda j, c: (0, j)),
        ),
        out_shape=jax.ShapeDtypeStruct((tokens, 2 * cols), mine.dtype),
        cost_estimate=pl.CostEstimate(
            flops=0, bytes_accessed=8 * tokens * cols, transcendentals=0
        ),
        compiler_params=pltpu.CompilerParams(vmem_limit_bytes=6 << 20),
    )(core, mine, other)


def join_kv_kernel(core_ref, *refs):
    own = pl.program_id(0) == core_ref[0]
    out_ref = refs[-1]

    @pl.when(own)
    def _():
        out_ref[0] = refs[0][...]
        out_ref[1] = refs[1][...]

    @pl.when(jnp.logical_not(own))
    def _():
        out_ref[0] = refs[2][...]
        out_ref[1] = refs[3][...]


def join_kv(core, key, value, other_key, other_value):
    tokens, cols = key.shape
    whole = pl.BlockSpec((tokens, cols), lambda j, c: (0, 0))
    return pl.pallas_call(
        join_kv_kernel,
        grid_spec=pltpu.PrefetchScalarGridSpec(
            num_scalar_prefetch=1,
            grid=(2,),
            in_specs=[whole] * 4,
            out_specs=pl.BlockSpec((2, tokens, cols), lambda j, c: (0, 0, j)),
        ),
        out_shape=jax.ShapeDtypeStruct((2, tokens, 2 * cols), key.dtype),
        cost_estimate=pl.CostEstimate(
            flops=0, bytes_accessed=16 * tokens * cols, transcendentals=0
        ),
        compiler_params=pltpu.CompilerParams(vmem_limit_bytes=8 << 20),
        name="join_kv",
    )(core, key, value, other_key, other_value)


def line_stages(nodes):
    stages = []
    span = 1
    while span < nodes:
        hops = [[] for _ in range(span)]
        place = [0] * nodes
        giver = [0] * nodes
        for base in range(0, nodes, 2 * span):
            middle = base + span
            for hop in range(span):
                below, above = middle - 1 - hop, middle + hop
                place[below] = place[above] = hop
                giver[below], giver[above] = middle, middle - 1
                if hop == 0:
                    hops[0] += [(above, below), (below, above)]
                else:
                    hops[hop] += [(below + 1, below), (above - 1, above)]
        stages.append((hops, place, giver))
        span *= 2
    return stages


class Rows:
    def __init__(self):
        self.count = lax.axis_size("rows")
        self.line = self.count // 2
        index = lax.axis_index("rows")
        self.node, self.side = index // 2, index % 2
        self.stages = line_stages(self.line)

    def across(self, value):
        return lax.ppermute(value, "rows", [(i, i ^ 1) for i in range(self.count)])

    def along(self, at, value):
        hops, place, _ = self.stages[at]
        chosen = None
        for hop, pairs in enumerate(hops):
            value = lax.ppermute(
                value, "rows", [(2 * a + s, 2 * b + s) for a, b in pairs for s in (0, 1)]
            )
            here = jnp.asarray(place, jnp.int32)[self.node] == hop
            chosen = value if chosen is None else jnp.where(here, value, chosen)
        return chosen

    def rest(self, pieces):
        found = []
        for at in range(1, len(self.stages)):
            found.append(self.along(at, jnp.concatenate(pieces)))
            pieces = pieces + [found[-1]]
        return found

    def nodes(self):
        held = [[n] for n in range(self.line)]
        for _, _, giver in self.stages:
            held = [held[n] + held[giver[n]] for n in range(self.line)]
        return jnp.asarray(held, jnp.int32)[self.node]


def block(tokens, stale_kv, stale_moments, norm_gain, norm_bias, w_query, w_key, w_value, w_out):
    _, band, width, chans = tokens.shape
    tok_count = band * width
    groups = stale_moments.shape[3]
    strips = lax.axis_size("strips")
    core = lax.axis_index("strips") % 2
    core_ids = core.astype(jnp.int32).reshape(1)
    half = w_query.shape[1] // 2
    rows = Rows()

    def swap(value, bits):
        return lax.ppermute(value, "strips", [(i, i ^ bits) for i in range(strips)])

    def half_of(value, which):
        return lax.dynamic_slice_in_dim(value, which * half, half, value.ndim - 1)

    own = {n: half_of(w, core)[None, None] for n, w in zip("qkvo", (w_query, w_key, w_value, w_out))}
    own_kv = jnp.concatenate([own["k"], own["v"]], axis=1)
    own_kvo = jnp.concatenate([own["k"], own["v"], own["o"]], axis=1)
    next_q = rows.along(0, own["q"])
    next_kvo = rows.along(0, own_kvo)
    next_of = {"q": next_q, **{n: next_kvo[:, i : i + 1] for i, n in enumerate("kvo")}}
    cross_q = rows.across(own["q"])
    cross_kv = rows.across(own_kv)
    cross_o = rows.across(own["o"])
    cross_of = {"q": (cross_q, 0), "k": (cross_kv, 0), "v": (cross_kv, 1), "o": (cross_o, 0)}
    pieces = {}
    for n in "qkvo":
        rest = rows.rest([own[n], next_of[n]])
        over = [rows.across(p) for p in [next_of[n], *rest]]
        at = "kvo".index(n) if n != "q" else 0
        pieces[n] = [(own[n], 0), (next_q if n == "q" else next_kvo, at)]
        pieces[n] += [(p, 0) for p in rest] + [cross_of[n]] + [(p, 0) for p in over]
    nodes = rows.nodes()
    ids = jnp.concatenate([nodes * 2 + rows.side, nodes * 2 + 1 - rows.side, core_ids])

    own_stale = stale_kv[0]
    own_moments = stale_moments[0, 0]
    near_moments = swap(own_moments, 1)
    far_moments = swap(own_moments + near_moments, 2)
    stale_other = half_of(own_stale, 1 - core)
    far_stale = swap(half_of(own_stale, core), 2)
    diag_stale = swap(stale_other, 3)
    near_stale = swap(stale_other, 1)

    flat = tokens.reshape(tok_count, chans)
    count = float(tok_count * strips * (chans // groups))
    fresh, normed = normalize(flat, near_moments + far_moments, norm_gain, norm_bias, count)
    normed_pair = swap(normed, 1)

    query = project(normed, normed_pair, pieces["q"], ids, 1.0 / HEAD**0.5)
    carry = attend_stale(core_ids, query, near_stale, own_stale, far_stale, diag_stale)
    key = project(normed, normed_pair, pieces["k"], ids)
    value = project(normed, normed_pair, pieces["v"], ids)
    other_key = swap(key[1], 1)
    other_value = swap(value[1], 1)
    heads = attend_fresh(query, key, value, carry)
    heads_pair = swap(heads, 1)
    fresh_kv = join_kv(core_ids, key[0], value[0], other_key, other_value)
    out = project(heads, heads_pair, pieces["o"], ids, split=True)
    attended = join(core_ids, out[0], swap(out[1], 1))
    return (
        attended.reshape(1, band, width, chans),
        fresh_kv[None],
        fresh[0][None, None],
        fresh[1][None, None],
    )


def solution(mesh):
    in_specs = (
        P("rows", None, "strips", None),
        P("rows", None, "strips", None),
        P("rows", "strips", None, None),
        P(),
        P(),
        P("rows", None),
        P("rows", None),
        P("rows", None),
        P("rows", None),
    )
    out_specs = (
        P("rows", None, "strips", None),
        P("rows", None, "strips", None),
        P("rows", "strips", None),
        P("rows", "strips", None),
    )
    return jax.shard_map(block, mesh=mesh, in_specs=in_specs, out_specs=out_specs, check_vma=False)
```

time: 422 us -> 154 us (0.36)
  matrix products: 186 us -> 0 us
  waiting for transfers between devices: 167 us -> 64.2 us
  Pallas kernels: 0 us -> 45 us
  starting transfers between devices: 0.19 us -> 27.9 us
  local copies, waits for them, and re-layouts: 21.4 us -> 7.47 us
  between operations: 14 us -> 1.63 us
  other arithmetic: 17.5 us -> 6.26 us
  blocking collectives: 8.4 us -> 0 us
    dot_general x124 -> x0, matrix products: 186 us -> none  [the longest x40 66.4 us: per_head(): jnp.dot(lower, head_vals, preferred_element_type=jnp.float32)]
    all_gather x5 -> x0, waiting for transfers between devices: 164 us -> none  [the longest x1 57.4 us: shards(): lax.all_gather(w_value, 'rows', axis=0, tiled=True)]
    ppermute x0 -> x31, waiting for transfers between devices: none -> 64.2 us  [the longest x10 24.2 us: swap(): return lax.ppermute(value, 'strips', [(i, i ^ bits) for i in range(strips)])]
    pallas_call x0 -> x9, Pallas kernels: none -> 45 us  [the longest x4 18.7 us: project(): pl.pallas_call(functools.partial(project_kernel, tuple((o for _, o in pie...]
    ppermute x0 -> x31, starting transfers between devices: none -> 27.9 us  [the longest x10 13.4 us: along(): lax.ppermute(value, 'rows', [(2 * a + s, 2 * b + s) for a, b in pairs for...]
    reduce_sum x43 -> x0, other arithmetic: 12.3 us -> none  [the longest x40 11.8 us: per_head(): head_total = head_total * factor + weights.sum(axis=-1)]
    psum x1 -> x0, blocking collectives: 8.4 us -> none  [shards(): totals = lax.psum(own_moments[0], 'strips')]
    concatenate x0 -> x7, other arithmetic: none -> 4.51 us  [the longest x4 3.48 us: rest(): found.append(self.along(at, jnp.concatenate(pieces)))]
  transfers between devices with their start and end apart: 5 -> 31, of which waited for: 3 -> 11; matrix products, arithmetic and copies ran while one was open for 53% -> 8% of each run, Pallas kernels for 0% -> 29%
where the time goes in v1:
time: 154 us; the launch traced here: 152 us
  waiting for transfers between devices  64.2 us (42%)
  Pallas kernels  45 us (29%)
  starting transfers between devices  27.9 us (18%)
  local copies, waits for them, and re-layouts  7.47 us (5%)
  other arithmetic  6.26 us (4%)
  between operations  1.63 us (1%)
    ppermute x10, waiting for transfers between devices, swap(): return lax.ppermute(value, 'strips', [(i, i ^ bits) for i in range(strips)])  24.2 us
    ppermute x11, waiting for transfers between devices, across(): return lax.ppermute(value, 'rows', [(i, i ^ 1) for i in range(self.count)])  22 us
    pallas_call x4, Pallas kernels, project(): pl.pallas_call(functools.partial(project_kernel, tuple((o for _, o in pie...  18.7 us
    ppermute x10, waiting for transfers between devices, along(): lax.ppermute(value, 'rows', [(2 * a + s, 2 * b + s) for a, b in pairs for...  18 us
    pallas_call x1, Pallas kernels, attend_stale(): pl.pallas_call(stale_kernel, grid_spec=pltpu.PrefetchScalarGridSpec(num_s...  14.2 us
    ppermute x10, starting transfers between devices, along(): lax.ppermute(value, 'rows', [(2 * a + s, 2 * b + s) for a, b in pairs for...  13.4 us
    ppermute x11, starting transfers between devices, across(): return lax.ppermute(value, 'rows', [(i, i ^ 1) for i in range(self.count)])  10.7 us
    pallas_call x1, Pallas kernels, attend_fresh(): pl.pallas_call(fresh_kernel, grid=(pairs,), in_specs=[flat] * 6 + [wide]...  7.34 us
  transfers between devices with their start and end apart: 31, of which 11 were waited for; matrix products, arithmetic and copies ran while one was open for 8% of the time, Pallas kernels for 29%

profile of v1, /device:TPU:0, one launch (start us, length us, event | category | flops | bytes accessed | tf_op | source)
XLA Modules:
  0.0 152.5 jit_solution(1810744201649570222)
XLA Ops:
  0.6 0.0 copy-start
  0.7 0.9 copy-done
  1.7 3.1 %collective-permute-start.3 = (bf16[1,1,160,640]{3,2,1,0:T(8,128)(2,1)S(1)}, bf16[1,1,160,640]{3,2,1,0:T(8,128)(2,1)S(1)}, u32[]{:S(2)}, u32[]{:S(2)}) collective-permute-start(bf16[1,1,160,640]{3,2,1,0:T(8,128)(2,1)S(1)} %dynamic-slice_bitcast_fusion.5.refs_3_), channel_id=1, source_target_pairs={{8,0},{12,4},{0,8},{4,12},{24,16},{28,20},{16,24},{20,28},{9,1},{1... | collective-permute-start | bytes 614408 | tf_op jit(solution)/shard_map/ppermute | solution.py:354
  4.8 0.9 dynamic-slice_bitcast_fusion.2.refs_3_
  5.7 1.1 dynamic-slice_bitcast_fusion.3
  6.8 0.9 pad_maximum_fusion
  7.7 0.0 collective-permute-start.9
  7.8 2.5 %collective-permute-done.3.refs_4_ = bf16[1,1,160,640]{3,2,1,0:T(8,128)(2,1)S(1)} collective-permute-done((bf16[1,1,160,640]{3,2,1,0:T(8,128)(2,1)S(1)}, bf16[1,1,160,640]{3,2,1,0:T(8,128)(2,1)S(1)}, u32[]{:S(2)}, u32[]{:S(2)}) %collective-permute-start.3) | collective-permute-done | bytes 204832 | tf_op jit(solution)/shard_map/ppermute | solution.py:354
  10.3 0.8 pad_maximum_fusion.1
  11.1 1.4 collective-permute-start.4
  12.5 1.4 collective-permute-start.6
  13.9 1.2 collective-permute-done
  15.1 1.5 collective-permute-start.1
  16.6 0.6 dynamic_slice.39
  17.8 0.8 collective-permute-done.1
  18.7 2.4 %normalize.1 = (f32[2,32]{1,0:T(2,128)S(1)}, bf16[384,1280]{1,0:T(8,128)(2,1)}) custom-call(bf16[384,1280]{1,0:T(8,128)(2,1)S(1)} %bitcast.29, f32[2,32]{1,0:T(2,128)S(1)} %add.52.other_ref, f32[1280]{0:T(1024)S(1)} %copy-done.3, f32[1280]{0:T(1024)S(1)} %copy-done.4), custom_call_target="tpu_custom_call" | custom-call | flops 3932160 | bytes 1966080 | tf_op jit(solution)/shard_map/normalize/pallas_call | solution.py:62
  21.1 0.6 collective-permute-start.7
  21.7 1.3 collective-permute-start.5
  23.0 0.4 collective-permute-done.9.refs_4_
  23.4 1.9 %fusion.1 = (bf16[1,1,160,640]{3,2,1,0:T(8,128)(2,1)}, bf16[1,1,160,640]{3,2,1,0:T(8,128)(2,1)S(1)}, bf16[1,1,160,640]{3,2,1,0:T(8,128)(2,1)S(1)}) fusion(bf16[1,3,160,640]{3,2,1,0:T(8,128)(2,1)} %collective-permute-done.9.refs_4_), kind=kLoop, calls=%fused_computation.24 | loop fusion | bytes 1228800 | tf_op jit(solution)/shard_map/slice | solution.py:396
  25.2 0.9 pad_maximum_fusion.2
  26.1 1.4 collective-permute-start.10
  27.5 0.8 pad_maximum_fusion.4
  28.4 8.3 %collective-permute-done.5 = bf16[2,1,160,640]{3,2,1,0:T(8,128)(2,1)S(1)} collective-permute-done((bf16[2,1,160,640]{3,2,1,0:T(8,128)(2,1)}, bf16[2,1,160,640]{3,2,1,0:T(8,128)(2,1)S(1)}, u32[]{:S(2)}, u32[]{:S(2)}) %collective-permute-start.5) | collective-permute-done | bytes 409632 | tf_op jit(solution)/shard_map/ppermute | solution.py:354
  36.7 1.4 collective-permute-start.15
  38.1 0.8 broadcast_select_fusion.3.refs_5_
  38.9 1.5 collective-permute-start.8
  40.4 1.5 dynamic-slice_bitcast_fusion
  41.9 1.3 collective-permute-start.11
  43.2 0.7 add_bitcast_fusion
  43.9 1.6 %collective-permute-start.21 = (bf16[2,384,640]{2,1,0:T(8,128)(2,1)}, bf16[2,384,640]{2,1,0:T(8,128)(2,1)S(1)}, u32[]{:S(2)}, u32[]{:S(2)}) collective-permute-start(bf16[2,384,640]{2,1,0:T(8,128)(2,1)} %get-tuple-element.31), channel_id=1, source_target_pairs={{0,3},{1,2},{2,1},{3,0},{4,7},{5,6},{6,5},{7,4},{8,11},{9,10},{10,... | collective-permute-start | bytes 2949128 | tf_op jit(solution)/shard_map/ppermute | solution.py:386
  45.5 0.5 collective-permute-start.20
  46.1 0.1 pad_add_fusion.refs_0_
  46.2 4.0 %collective-permute-done.8.refs_8_ = bf16[2,1,160,640]{3,2,1,0:T(8,128)(2,1)} collective-permute-done((bf16[2,1,160,640]{3,2,1,0:T(8,128)(2,1)}, bf16[2,1,160,640]{3,2,1,0:T(8,128)(2,1)}, u32[]{:S(2)}, u32[]{:S(2)}) %collective-permute-start.8) | collective-permute-done | bytes 409632 | tf_op jit(solution)/shard_map/ppermute | solution.py:348
  50.1 1.3 collective-permute-start.16
  51.4 1.0 pad_maximum_fusion.5
  52.4 2.9 %collective-permute-done.11 = bf16[2,1,160,640]{3,2,1,0:T(8,128)(2,1)S(1)} collective-permute-done((bf16[2,1,160,640]{3,2,1,0:T(8,128)(2,1)}, bf16[2,1,160,640]{3,2,1,0:T(8,128)(2,1)S(1)}, u32[]{:S(2)}, u32[]{:S(2)}) %collective-permute-start.11) | collective-permute-done | bytes 409632 | tf_op jit(solution)/shard_map/ppermute | solution.py:354
  55.3 0.4 collective-permute-start.12
  55.8 4.5 %shard_map.165 = (bf16[384,640]{1,0:T(8,128)(2,1)S(1)}, bf16[384,640]{1,0:T(8,128)(2,1)S(1)}) custom-call(s32[9]{0:T(128)S(1)} %pad_add_fusion.refs_0_, bf16[384,1280]{1,0:T(8,128)(2,1)} %get-tuple-element.17.refs_1_, bf16[384,1280]{1,0:T(8,128)(2,1)} %collective-permute-done.2.refs_2_, bf16[1,1,160,640]{3,2,1,0:T(8,128)(2,1)S(1)} %dynamic-slice_bitcast_fusion.5.refs_3_, ...), custom_call_target="tpu_custom_call" | custom-call | flops 1258291200 | bytes 3604480 | tf_op jit(solution)/shard_map/pallas_call | solution.py:139
  60.3 3.9 %collective-permute-done.16 = bf16[2,1,160,640]{3,2,1,0:T(8,128)(2,1)S(1)} collective-permute-done((bf16[2,1,160,640]{3,2,1,0:T(8,128)(2,1)}, bf16[2,1,160,640]{3,2,1,0:T(8,128)(2,1)S(1)}, u32[]{:S(2)}, u32[]{:S(2)}) %collective-permute-start.16) | collective-permute-done | bytes 409632 | tf_op jit(solution)/shard_map/ppermute | solution.py:354
  64.2 1.6 %collective-permute-start.13 = (bf16[1,1,160,640]{3,2,1,0:T(8,128)(2,1)S(1)}, bf16[1,1,160,640]{3,2,1,0:T(8,128)(2,1)S(1)}, u32[]{:S(2)}, u32[]{:S(2)}) collective-permute-start(bf16[1,1,160,640]{3,2,1,0:T(8,128)(2,1)S(1)} %copy-done.9), channel_id=1, source_target_pairs={{0,4},{4,0},{8,12},{12,8},{16,20},{20,16},{24,28},{28,24},{1,5},{5... | collective-permute-start | bytes 614408 | tf_op jit(solution)/shard_map/ppermute | solution.py:348
  65.8 0.1 broadcast_select_fusion.1.refs_5_
  66.0 0.5 collective-permute-start.17
  66.4 0.7 collective-permute-start.23
  67.1 22.2 %collective-permute-done.20.far_ref = bf16[2,384,640]{2,1,0:T(8,128)(2,1)S(1)} collective-permute-done((bf16[2,384,640]{2,1,0:T(8,128)(2,1)}, bf16[2,384,640]{2,1,0:T(8,128)(2,1)S(1)}, u32[]{:S(2)}, u32[]{:S(2)}) %collective-permute-start.20) | collective-permute-done | bytes 983072 | tf_op jit(solution)/shard_map/ppermute | solution.py:386
  89.3 0.5 collective-permute-start.14
  89.9 1.5 collective-permute-start.18
  91.4 14.2 %attend_stale.1 = (f32[2,384,640]{2,1,0:T(8,128)S(1)}, f32[2,384,640]{2,1,0:T(8,128)S(1)}, f32[2,384,640]{2,1,0:T(8,128)S(1)}) custom-call(s32[1]{0:T(128)} %bitcast.core_ref, bf16[384,640]{1,0:T(8,128)(2,1)S(1)} %get-tuple-element.18.q0_ref, bf16[384,640]{1,0:T(8,128)(2,1)S(1)} %get-tuple-element.19.q1_ref, ...), custom_call_target="tpu_custom_call" | custom-call | flops 9059696640 | bytes 9830400 | tf_op jit(solution)/shard_map/attend_stale/pallas_call | solution.py:211
  105.6 1.5 collective-permute-start.24
  107.1 4.4 %shard_map.166 = (bf16[384,640]{1,0:T(8,128)(2,1)S(1)}, bf16[384,640]{1,0:T(8,128)(2,1)S(1)}) custom-call(s32[9]{0:T(128)S(1)} %pad_add_fusion.refs_0_, bf16[384,1280]{1,0:T(8,128)(2,1)} %get-tuple-element.17.refs_1_, bf16[384,1280]{1,0:T(8,128)(2,1)} %collective-permute-done.2.refs_2_, bf16[1,1,160,640]{3,2,1,0:T(8,128)(2,1)S(1)} %get-tuple-element.40.refs_3_, ...), custom_call_target="tpu_custom_call" | custom-call | flops 1258291200 | bytes 3604480 | tf_op jit(solution)/shard_map/pallas_call | solution.py:139
  111.6 4.4 %shard_map.167 = (bf16[384,640]{1,0:T(8,128)(2,1)S(1)}, bf16[384,640]{1,0:T(8,128)(2,1)S(1)}) custom-call(s32[9]{0:T(128)S(1)} %pad_add_fusion.refs_0_, bf16[384,1280]{1,0:T(8,128)(2,1)} %get-tuple-element.17.refs_1_, bf16[384,1280]{1,0:T(8,128)(2,1)} %collective-permute-done.2.refs_2_, bf16[1,1,160,640]{3,2,1,0:T(8,128)(2,1)S(1)} %get-tuple-element.39.refs_3_, ...), custom_call_target="tpu_custom_call" | custom-call | flops 1258291200 | bytes 3604480 | tf_op jit(solution)/shard_map/pallas_call | solution.py:139
  116.0 7.3 %attend_fresh.1.refs_1_ = bf16[2,384,640]{2,1,0:T(8,128)(2,1)S(1)} custom-call(bf16[384,640]{1,0:T(8,128)(2,1)S(1)} %get-tuple-element.18.q0_ref, bf16[384,640]{1,0:T(8,128)(2,1)S(1)} %get-tuple-element.19.q1_ref, bf16[384,640]{1,0:T(8,128)(2,1)S(1)} %get-tuple-element.20.k0_ref.refs_0_, bf16[384,640]{1,0:T(8,128)(2,1)S(1)} %get-tuple-element.21.k1_ref, ...), custom_call_target="tpu_custom_call" | custom-call | flops 3019898880 | bytes 9830400 | tf_op jit(solution)/shard_map/attend_fresh/pallas_call | solution.py:235
  123.4 0.1 collective-permute-start.22
  123.4 0.1 broadcast_select_fusion.refs_5_
  123.5 0.6 collective-permute-start.27
  124.1 1.5 collective-permute-start.25
  125.6 0.5 collective-permute-start.26
  126.1 14.2 %collective-permute-done.25.refs_6_ = bf16[1,1,160,640]{3,2,1,0:T(8,128)(2,1)S(1)} collective-permute-done((bf16[1,1,160,640]{3,2,1,0:T(8,128)(2,1)S(1)}, bf16[1,1,160,640]{3,2,1,0:T(8,128)(2,1)S(1)}, u32[]{:S(2)}, u32[]{:S(2)}) %collective-permute-start.25) | collective-permute-done | bytes 204832 | tf_op jit(solution)/shard_map/ppermute | solution.py:348
  140.3 3.9 %collective-permute-done.26.refs_7_ = bf16[1,1,160,640]{3,2,1,0:T(8,128)(2,1)S(1)} collective-permute-done((bf16[1,1,160,640]{3,2,1,0:T(8,128)(2,1)S(1)}, bf16[1,1,160,640]{3,2,1,0:T(8,128)(2,1)S(1)}, u32[]{:S(2)}, u32[]{:S(2)}) %collective-permute-start.26) | collective-permute-done | bytes 204832 | tf_op jit(solution)/shard_map/ppermute | solution.py:348
  144.2 5.3 %shard_map.168 = (bf16[384,640]{1,0:T(8,128)(2,1)S(1)}, bf16[384,640]{1,0:T(8,128)(2,1)S(1)}) custom-call(s32[9]{0:T(128)S(1)} %pad_add_fusion.refs_0_, bf16[2,384,640]{2,1,0:T(8,128)(2,1)S(1)} %attend_fresh.1.refs_1_, bf16[2,384,640]{2,1,0:T(8,128)(2,1)S(1)} %collective-permute-done.22.refs_2_, ...), custom_call_target="tpu_custom_call" | custom-call | flops 1258291200 | bytes 3604480 | tf_op jit(solution)/shard_map/pallas_call | solution.py:139
  149.5 0.1 collective-permute-start.28
  149.6 0.5 slice_bitcast_fusion
  150.1 1.4 join_kv.1
  151.5 1.0 shard_map.169
  (52 shorter events, 0.2 us)
Async XLA Ops:
  0.6 1.0 copy-start
  0.6 16.0 %copy-start.11 = (s32[4]{0:T(128)S(1)}, s32[4]{0:T(128)}, u32[]{:S(2)}) copy-start(s32[4]{0:T(128)} %constant.58.clone) | copy-start | bytes 52
  0.7 13.3 %copy-start.10 = (f32[1,1,2,32]{3,2,1,0:T(2,128)S(1)}, f32[1,1,2,32]{3,2,1,0:T(2,128)}, u32[]{:S(2)}) copy-start(f32[1,1,2,32]{3,2,1,0:T(2,128)} %param.16) | copy-start | bytes 772
  0.7 18.0 %copy-start.2 = (bf16[1,24,16,1280]{3,2,1,0:T(8,128)(2,1)S(1)}, bf16[1,24,16,1280]{3,2,1,0:T(8,128)(2,1)}, u32[]{:S(2)}) copy-start(bf16[1,24,16,1280]{3,2,1,0:T(8,128)(2,1)} %param.14) | copy-start | bytes 2949124
  0.7 18.0 %copy-start.3 = (f32[1280]{0:T(1024)S(1)}, f32[1280]{0:T(1024)}, u32[]{:S(2)}) copy-start(f32[1280]{0:T(1024)} %gain_ref.1) | copy-start | bytes 15364
  0.7 18.0 %copy-start.4 = (f32[1280]{0:T(1024)S(1)}, f32[1280]{0:T(1024)}, u32[]{:S(2)}) copy-start(f32[1280]{0:T(1024)} %bias_ref.1) | copy-start | bytes 15364
  1.7 8.6 %collective-permute-start.3 = (bf16[1,1,160,640]{3,2,1,0:T(8,128)(2,1)S(1)}, bf16[1,1,160,640]{3,2,1,0:T(8,128)(2,1)S(1)}, u32[]{:S(2)}, u32[]{:S(2)}) collective-permute-start(bf16[1,1,160,640]{3,2,1,0:T(8,128)(2,1)S(1)} %dynamic-slice_bitcast_fusion.5.refs_3_), channel_id=1, source_target_pairs={{8,0},{12,4},{0,8},{4,12},{24,16},{28,20},{16,24},{20,28},{9,1},{1... | collective-permute-start | bytes 614408 | tf_op jit(solution)/shard_map/ppermute | solution.py:354
  7.7 15.6 %collective-permute-start.9 = (bf16[1,3,160,640]{3,2,1,0:T(8,128)(2,1)}, bf16[1,3,160,640]{3,2,1,0:T(8,128)(2,1)}, u32[]{:S(2)}, u32[]{:S(2)}) collective-permute-start(bf16[1,3,160,640]{3,2,1,0:T(8,128)(2,1)} %pad_maximum_fusion), channel_id=1, source_target_pairs={{8,0},{12,4},{0,8},{4,12},{24,16},{28,20},{16,24},{20,28},{9,1},{1... | collective-permute-start | bytes 1843208 | tf_op jit(solution)/shard_map/ppermute | solution.py:354
  11.1 10.6 %collective-permute-start.4 = (bf16[2,1,160,640]{3,2,1,0:T(8,128)(2,1)}, bf16[2,1,160,640]{3,2,1,0:T(8,128)(2,1)}, u32[]{:S(2)}, u32[]{:S(2)}) collective-permute-start(bf16[2,1,160,640]{3,2,1,0:T(8,128)(2,1)} %pad_maximum_fusion.1), channel_id=1, source_target_pairs={{16,8},{20,12},{8,16},{12,20},{17,9},{21,13},{9,17},{13,21},{18,10... | collective-permute-start | bytes 1228808 | tf_op jit(solution)/shard_map/ppermute | solution.py:354
  12.5 26.5 %collective-permute-start.6 = (bf16[1,1,160,640]{3,2,1,0:T(8,128)(2,1)S(1)}, bf16[1,1,160,640]{3,2,1,0:T(8,128)(2,1)}, u32[]{:S(2)}, u32[]{:S(2)}) collective-permute-start(bf16[1,1,160,640]{3,2,1,0:T(8,128)(2,1)S(1)} %dynamic-slice_bitcast_fusion.5.refs_3_), channel_id=1, source_target_pairs={{0,4},{4,0},{8,12},{12,8},{16,20},{20,16},{24,28},{28,24},{1,5},{5... | collective-permute-start | bytes 614408 | tf_op jit(solution)/shard_map/ppermute | solution.py:348
  13.9 1.2 collective-permute-start
  15.1 3.6 %collective-permute-start.1 = (f32[2,32]{1,0:T(2,128)S(1)}, f32[2,32]{1,0:T(2,128)S(1)}, u32[]{:S(2)}, u32[]{:S(2)}) collective-permute-start(f32[2,32]{1,0:T(2,128)S(1)} %bitcast_add_fusion), channel_id=1, source_target_pairs={{0,2},{1,3},{2,0},{3,1},{4,6},{5,7},{6,4},{7,5},{8,10},{9,11},{10,... | collective-permute-start | bytes 776 | tf_op jit(solution)/shard_map/ppermute | solution.py:386
  21.1 19.4 %copy-start.1 = (bf16[1,2,384,1280]{3,2,1,0:T(8,128)(2,1)S(1)}, bf16[1,2,384,1280]{3,2,1,0:T(8,128)(2,1)}, u32[]{:S(2)}) copy-start(bf16[1,2,384,1280]{3,2,1,0:T(8,128)(2,1)} %param.15) | copy-start | bytes 5898244
  21.1 22.8 %collective-permute-start.2 = (bf16[384,1280]{1,0:T(8,128)(2,1)}, bf16[384,1280]{1,0:T(8,128)(2,1)}, u32[]{:S(2)}, u32[]{:S(2)}) collective-permute-start(bf16[384,1280]{1,0:T(8,128)(2,1)} %get-tuple-element.17.refs_1_), channel_id=1, source_target_pairs={{0,1},{1,0},{2,3},{3,2},{4,5},{5,4},{6,7},{7,6},{8,9},{9,8},{10,11... | collective-permute-start | bytes 2949128 | tf_op jit(solution)/shard_map/ppermute | solution.py:386
  21.1 22.8 %collective-permute-start.7 = (bf16[1,1,160,640]{3,2,1,0:T(8,128)(2,1)S(1)}, bf16[1,1,160,640]{3,2,1,0:T(8,128)(2,1)}, u32[]{:S(2)}, u32[]{:S(2)}) collective-permute-start(bf16[1,1,160,640]{3,2,1,0:T(8,128)(2,1)S(1)} %collective-permute-done.3.refs_4_), channel_id=1, source_target_pairs={{0,4},{4,0},{8,12},{12,8},{16,20},{20,16},{24,28},{28,24},{1,5},{5... | collective-permute-start | bytes 614408 | tf_op jit(solution)/shard_map/ppermute | solution.py:348
  21.7 15.0 %collective-permute-start.5 = (bf16[2,1,160,640]{3,2,1,0:T(8,128)(2,1)}, bf16[2,1,160,640]{3,2,1,0:T(8,128)(2,1)S(1)}, u32[]{:S(2)}, u32[]{:S(2)}) collective-permute-start(bf16[2,1,160,640]{3,2,1,0:T(8,128)(2,1)} %collective-permute-done.4), channel_id=1, source_target_pairs={{8,0},{12,4},{16,24},{20,28},{9,1},{13,5},{17,25},{21,29},{10,2},{... | collective-permute-start | bytes 1228808 | tf_op jit(solution)/shard_map/ppermute | solution.py:354
  25.2 2.3 %copy-start.6 = (bf16[1,1,160,640]{3,2,1,0:T(8,128)(2,1)}, bf16[1,1,160,640]{3,2,1,0:T(8,128)(2,1)S(1)}, u32[]{:S(2)}) copy-start(bf16[1,1,160,640]{3,2,1,0:T(8,128)(2,1)S(1)} %get-tuple-element.33) | copy-start | bytes 614404
  25.2 3.1 %copy-start.8 = (bf16[1,1,160,640]{3,2,1,0:T(8,128)(2,1)}, bf16[1,1,160,640]{3,2,1,0:T(8,128)(2,1)S(1)}, u32[]{:S(2)}) copy-start(bf16[1,1,160,640]{3,2,1,0:T(8,128)(2,1)S(1)} %get-tuple-element.34) | copy-start | bytes 614404
  26.1 15.8 %collective-permute-start.10 = (bf16[2,1,160,640]{3,2,1,0:T(8,128)(2,1)}, bf16[2,1,160,640]{3,2,1,0:T(8,128)(2,1)}, u32[]{:S(2)}, u32[]{:S(2)}) collective-permute-start(bf16[2,1,160,640]{3,2,1,0:T(8,128)(2,1)} %pad_maximum_fusion.2), channel_id=1, source_target_pairs={{16,8},{20,12},{8,16},{12,20},{17,9},{21,13},{9,17},{13,21},{18,10... | collective-permute-start | bytes 1228808 | tf_op jit(solution)/shard_map/ppermute | solution.py:354
  36.7 8.9 %collective-permute-start.15 = (bf16[2,1,160,640]{3,2,1,0:T(8,128)(2,1)}, bf16[2,1,160,640]{3,2,1,0:T(8,128)(2,1)}, u32[]{:S(2)}, u32[]{:S(2)}) collective-permute-start(bf16[2,1,160,640]{3,2,1,0:T(8,128)(2,1)} %pad_maximum_fusion.4), channel_id=1, source_target_pairs={{16,8},{20,12},{8,16},{12,20},{17,9},{21,13},{9,17},{13,21},{18,10... | collective-permute-start | bytes 1228808 | tf_op jit(solution)/shard_map/ppermute | solution.py:354
  38.9 11.2 %collective-permute-start.8 = (bf16[2,1,160,640]{3,2,1,0:T(8,128)(2,1)}, bf16[2,1,160,640]{3,2,1,0:T(8,128)(2,1)}, u32[]{:S(2)}, u32[]{:S(2)}) collective-permute-start(bf16[2,1,160,640]{3,2,1,0:T(8,128)(2,1)} %broadcast_select_fusion.3.refs_5_), channel_id=1, source_target_pairs={{0,4},{4,0},{8,12},{12,8},{16,20},{20,16},{24,28},{28,24},{1,5},{5... | collective-permute-start | bytes 1228808 | tf_op jit(solution)/shard_map/ppermute | solution.py:348
  41.9 13.4 %collective-permute-start.11 = (bf16[2,1,160,640]{3,2,1,0:T(8,128)(2,1)}, bf16[2,1,160,640]{3,2,1,0:T(8,128)(2,1)S(1)}, u32[]{:S(2)}, u32[]{:S(2)}) collective-permute-start(bf16[2,1,160,640]{3,2,1,0:T(8,128)(2,1)} %collective-permute-done.10), channel_id=1, source_target_pairs={{8,0},{12,4},{16,24},{20,28},{9,1},{13,5},{17,25},{21,29},{10,2},{... | collective-permute-start | bytes 1228808 | tf_op jit(solution)/shard_map/ppermute | solution.py:354
  43.9 22.5 %collective-permute-start.19 = (bf16[2,384,640]{2,1,0:T(8,128)(2,1)}, bf16[2,384,640]{2,1,0:T(8,128)(2,1)S(1)}, u32[]{:S(2)}, u32[]{:S(2)}) collective-permute-start(bf16[2,384,640]{2,1,0:T(8,128)(2,1)} %get-tuple-element.31), channel_id=1, source_target_pairs={{0,1},{1,0},{2,3},{3,2},{4,5},{5,4},{6,7},{7,6},{8,9},{9,8},{10,11... | collective-permute-start | bytes 2949128 | tf_op jit(solution)/shard_map/ppermute | solution.py:386
  43.9 45.9 %collective-permute-start.21 = (bf16[2,384,640]{2,1,0:T(8,128)(2,1)}, bf16[2,384,640]{2,1,0:T(8,128)(2,1)S(1)}, u32[]{:S(2)}, u32[]{:S(2)}) collective-permute-start(bf16[2,384,640]{2,1,0:T(8,128)(2,1)} %get-tuple-element.31), channel_id=1, source_target_pairs={{0,3},{1,2},{2,1},{3,0},{4,7},{5,6},{6,5},{7,4},{8,11},{9,10},{10,... | collective-permute-start | bytes 2949128 | tf_op jit(solution)/shard_map/ppermute | solution.py:386
  45.5 43.8 %collective-permute-start.20 = (bf16[2,384,640]{2,1,0:T(8,128)(2,1)}, bf16[2,384,640]{2,1,0:T(8,128)(2,1)S(1)}, u32[]{:S(2)}, u32[]{:S(2)}) collective-permute-start(bf16[2,384,640]{2,1,0:T(8,128)(2,1)} %get-tuple-element.30), channel_id=1, source_target_pairs={{0,2},{1,3},{2,0},{3,1},{4,6},{5,7},{6,4},{7,5},{8,10},{9,11},{10,... | collective-permute-start | bytes 2949128 | tf_op jit(solution)/shard_map/ppermute | solution.py:386
  50.1 14.1 %collective-permute-start.16 = (bf16[2,1,160,640]{3,2,1,0:T(8,128)(2,1)}, bf16[2,1,160,640]{3,2,1,0:T(8,128)(2,1)S(1)}, u32[]{:S(2)}, u32[]{:S(2)}) collective-permute-start(bf16[2,1,160,640]{3,2,1,0:T(8,128)(2,1)} %collective-permute-done.15), channel_id=1, source_target_pairs={{8,0},{12,4},{16,24},{20,28},{9,1},{13,5},{17,25},{21,29},{10,2},{... | collective-permute-start | bytes 1228808 | tf_op jit(solution)/shard_map/ppermute | solution.py:354
  55.3 10.7 %collective-permute-start.12 = (bf16[1,2,160,640]{3,2,1,0:T(8,128)(2,1)S(1)}, bf16[1,2,160,640]{3,2,1,0:T(8,128)(2,1)S(1)}, u32[]{:S(2)}, u32[]{:S(2)}) collective-permute-start(bf16[1,2,160,640]{3,2,1,0:T(8,128)(2,1)S(1)} %pad_maximum_fusion.3), channel_id=1, source_target_pairs={{0,4},{4,0},{8,12},{12,8},{16,20},{20,16},{24,28},{28,24},{1,5},{5... | collective-permute-start | bytes 1228808 | tf_op jit(solution)/shard_map/ppermute | solution.py:348
  55.7 8.5 %copy-start.9 = (bf16[1,1,160,640]{3,2,1,0:T(8,128)(2,1)S(1)}, bf16[1,1,160,640]{3,2,1,0:T(8,128)(2,1)}, u32[]{:S(2)}) copy-start(bf16[1,1,160,640]{3,2,1,0:T(8,128)(2,1)} %copy-done.8) | copy-start | bytes 614404
  55.7 10.2 %copy-start.7 = (bf16[1,1,160,640]{3,2,1,0:T(8,128)(2,1)S(1)}, bf16[1,1,160,640]{3,2,1,0:T(8,128)(2,1)}, u32[]{:S(2)}) copy-start(bf16[1,1,160,640]{3,2,1,0:T(8,128)(2,1)} %copy-done.6) | copy-start | bytes 614404
  64.2 42.8 %collective-permute-start.13 = (bf16[1,1,160,640]{3,2,1,0:T(8,128)(2,1)S(1)}, bf16[1,1,160,640]{3,2,1,0:T(8,128)(2,1)S(1)}, u32[]{:S(2)}, u32[]{:S(2)}) collective-permute-start(bf16[1,1,160,640]{3,2,1,0:T(8,128)(2,1)S(1)} %copy-done.9), channel_id=1, source_target_pairs={{0,4},{4,0},{8,12},{12,8},{16,20},{20,16},{24,28},{28,24},{1,5},{5... | collective-permute-start | bytes 614408 | tf_op jit(solution)/shard_map/ppermute | solution.py:348
  66.0 45.6 %collective-permute-start.17 = (bf16[1,1,160,640]{3,2,1,0:T(8,128)(2,1)S(1)}, bf16[1,1,160,640]{3,2,1,0:T(8,128)(2,1)S(1)}, u32[]{:S(2)}, u32[]{:S(2)}) collective-permute-start(bf16[1,1,160,640]{3,2,1,0:T(8,128)(2,1)S(1)} %copy-done.7), channel_id=1, source_target_pairs={{0,4},{4,0},{8,12},{12,8},{16,20},{20,16},{24,28},{28,24},{1,5},{5... | collective-permute-start | bytes 614408 | tf_op jit(solution)/shard_map/ppermute | solution.py:348
  66.4 39.1 %collective-permute-start.23 = (bf16[2,1,160,640]{3,2,1,0:T(8,128)(2,1)S(1)}, bf16[2,1,160,640]{3,2,1,0:T(8,128)(2,1)S(1)}, u32[]{:S(2)}, u32[]{:S(2)}) collective-permute-start(bf16[2,1,160,640]{3,2,1,0:T(8,128)(2,1)S(1)} %pad_maximum_fusion.5), channel_id=1, source_target_pairs={{16,8},{20,12},{8,16},{12,20},{17,9},{21,13},{9,17},{13,21},{18,10... | collective-permute-start | bytes 1228808 | tf_op jit(solution)/shard_map/ppermute | solution.py:354
  89.3 17.8 %collective-permute-start.14 = (bf16[2,1,160,640]{3,2,1,0:T(8,128)(2,1)S(1)}, bf16[2,1,160,640]{3,2,1,0:T(8,128)(2,1)S(1)}, u32[]{:S(2)}, u32[]{:S(2)}) collective-permute-start(bf16[2,1,160,640]{3,2,1,0:T(8,128)(2,1)S(1)} %broadcast_select_fusion.2.refs_5_), channel_id=1, source_target_pairs={{0,4},{4,0},{8,12},{12,8},{16,20},{20,16},{24,28},{28,24},{1,5},{5... | collective-permute-start | bytes 1228808 | tf_op jit(solution)/shard_map/ppermute | solution.py:348
  89.9 21.7 %collective-permute-start.18 = (bf16[2,1,160,640]{3,2,1,0:T(8,128)(2,1)S(1)}, bf16[2,1,160,640]{3,2,1,0:T(8,128)(2,1)S(1)}, u32[]{:S(2)}, u32[]{:S(2)}) collective-permute-start(bf16[2,1,160,640]{3,2,1,0:T(8,128)(2,1)S(1)} %broadcast_select_fusion.1.refs_5_), channel_id=1, source_target_pairs={{0,4},{4,0},{8,12},{12,8},{16,20},{20,16},{24,28},{28,24},{1,5},{5... | collective-permute-start | bytes 1228808 | tf_op jit(solution)/shard_map/ppermute | solution.py:348
  105.6 17.9 %collective-permute-start.24 = (bf16[2,1,160,640]{3,2,1,0:T(8,128)(2,1)S(1)}, bf16[2,1,160,640]{3,2,1,0:T(8,128)(2,1)S(1)}, u32[]{:S(2)}, u32[]{:S(2)}) collective-permute-start(bf16[2,1,160,640]{3,2,1,0:T(8,128)(2,1)S(1)} %collective-permute-done.23), channel_id=1, source_target_pairs={{8,0},{12,4},{16,24},{20,28},{9,1},{13,5},{17,25},{21,29},{10,2},{... | collective-permute-start | bytes 1228808 | tf_op jit(solution)/shard_map/ppermute | solution.py:354
  116.0 9.6 %copy-start.5 = (bf16[1,1,160,640]{3,2,1,0:T(8,128)(2,1)S(1)}, bf16[1,1,160,640]{3,2,1,0:T(8,128)(2,1)}, u32[]{:S(2)}) copy-start(bf16[1,1,160,640]{3,2,1,0:T(8,128)(2,1)} %get-tuple-element.32) | copy-start | bytes 614404
  123.4 20.9 %collective-permute-start.22 = (bf16[2,384,640]{2,1,0:T(8,128)(2,1)S(1)}, bf16[2,384,640]{2,1,0:T(8,128)(2,1)S(1)}, u32[]{:S(2)}, u32[]{:S(2)}) collective-permute-start(bf16[2,384,640]{2,1,0:T(8,128)(2,1)S(1)} %attend_fresh.1.refs_1_), channel_id=1, source_target_pairs={{0,1},{1,0},{2,3},{3,2},{4,5},{5,4},{6,7},{7,6},{8,9},{9,8},{10,11... | collective-permute-start | bytes 2949128 | tf_op jit(solution)/shard_map/ppermute | solution.py:386
  123.5 20.7 %collective-permute-start.27 = (bf16[2,1,160,640]{3,2,1,0:T(8,128)(2,1)S(1)}, bf16[2,1,160,640]{3,2,1,0:T(8,128)(2,1)S(1)}, u32[]{:S(2)}, u32[]{:S(2)}) collective-permute-start(bf16[2,1,160,640]{3,2,1,0:T(8,128)(2,1)S(1)} %broadcast_select_fusion.refs_5_), channel_id=1, source_target_pairs={{0,4},{4,0},{8,12},{12,8},{16,20},{20,16},{24,28},{28,24},{1,5},{5... | collective-permute-start | bytes 1228808 | tf_op jit(solution)/shard_map/ppermute | solution.py:348
  124.1 16.2 %collective-permute-start.25 = (bf16[1,1,160,640]{3,2,1,0:T(8,128)(2,1)S(1)}, bf16[1,1,160,640]{3,2,1,0:T(8,128)(2,1)S(1)}, u32[]{:S(2)}, u32[]{:S(2)}) collective-permute-start(bf16[1,1,160,640]{3,2,1,0:T(8,128)(2,1)S(1)} %dynamic-slice_bitcast_fusion.2.refs_3_), channel_id=1, source_target_pairs={{0,4},{4,0},{8,12},{12,8},{16,20},{20,16},{24,28},{28,24},{1,5},{5... | collective-permute-start | bytes 614408 | tf_op jit(solution)/shard_map/ppermute | solution.py:348
  125.6 18.6 %collective-permute-start.26 = (bf16[1,1,160,640]{3,2,1,0:T(8,128)(2,1)S(1)}, bf16[1,1,160,640]{3,2,1,0:T(8,128)(2,1)S(1)}, u32[]{:S(2)}, u32[]{:S(2)}) collective-permute-start(bf16[1,1,160,640]{3,2,1,0:T(8,128)(2,1)S(1)} %copy-done.5), channel_id=1, source_target_pairs={{0,4},{4,0},{8,12},{12,8},{16,20},{20,16},{24,28},{28,24},{1,5},{5... | collective-permute-start | bytes 614408 | tf_op jit(solution)/shard_map/ppermute | solution.py:348
  126.1 24.0 %collective-permute-start.29 = (bf16[384,640]{1,0:T(8,128)(2,1)S(1)}, bf16[384,640]{1,0:T(8,128)(2,1)S(1)}, u32[]{:S(2)}, u32[]{:S(2)}) collective-permute-start(bf16[384,640]{1,0:T(8,128)(2,1)S(1)} %get-tuple-element.21.k1_ref), channel_id=1, source_target_pairs={{0,1},{1,0},{2,3},{3,2},{4,5},{5,4},{6,7},{7,6},{8,9},{9,8},{10,11... | collective-permute-start | bytes 1474568 | tf_op jit(solution)/shard_map/ppermute | solution.py:386
  140.3 9.8 %collective-permute-start.30 = (bf16[384,640]{1,0:T(8,128)(2,1)S(1)}, bf16[384,640]{1,0:T(8,128)(2,1)S(1)}, u32[]{:S(2)}, u32[]{:S(2)}) collective-permute-start(bf16[384,640]{1,0:T(8,128)(2,1)S(1)} %get-tuple-element.23.v1_ref), channel_id=1, source_target_pairs={{0,1},{1,0},{2,3},{3,2},{4,5},{5,4},{6,7},{7,6},{8,9},{9,8},{10,11... | collective-permute-start | bytes 1474568 | tf_op jit(solution)/shard_map/ppermute | solution.py:386
  149.5 2.0 %collective-permute-start.28 = (bf16[384,640]{1,0:T(8,128)(2,1)S(1)}, bf16[384,640]{1,0:T(8,128)(2,1)S(1)}, u32[]{:S(2)}, u32[]{:S(2)}) collective-permute-start(bf16[384,640]{1,0:T(8,128)(2,1)S(1)} %get-tuple-element.28), channel_id=1, source_target_pairs={{0,1},{1,0},{2,3},{3,2},{4,5},{5,4},{6,7},{7,6},{8,9},{9,8},{10,11... | collective-permute-start | bytes 1474568 | tf_op jit(solution)/shard_map/ppermute | solution.py:386
